TPU v7x, 512 devices: a whole 4x4x16 slice. The times are simulated.
512 devices in a mesh: rep: 8 (over y, core), ep: 64 (over x, z).
Axes of the slice: x: 4, y: 4, z: 16, core: 2. Of those that a mesh axis runs over, the one named last changes fastest.
Arguments:
- hidden_state: bfloat16 [1024, 4096], P(('ep', 'rep')), may hold values from -6 to 6
- norm_gain: float32 [4096], replicated, may hold values from 0.5 to 1.5
- expert_ids: int32 [1024, 8], P('ep'), may hold values from 0 to 63, as said below
- gate_logits: float32 [1024, 8], P('ep'), may hold values from -4 to 4
- gate_weight: bfloat16 [64, 4096, 1024], P('ep', None, 'rep'), may hold values from -0.09375 to 0.09375
- up_weight: bfloat16 [64, 4096, 1024], P('ep', None, 'rep'), may hold values from -0.09375 to 0.09375
- down_weight: bfloat16 [64, 1024, 4096], P('ep', 'rep'), may hold values from -0.1875 to 0.1875
Outputs:
- moe_out: bfloat16 [1024, 4096], P(('ep', 'rep'))
Inputs may be any that keep to these rules, and one draw needn't show every extreme that they name: `expert_ids`: in each aligned block of 16 rows, each row names 8 different experts; two experts, the same in every block, are each named by exactly 9 rows of the block; every other expert by at most 2 rows of a block, a bound reached in every block.
All inputs are finite; a program needn't handle non-finite values.
Results may differ from a plain program's by a relative error of at most 0.0065.
Values may be sent and summed in bfloat16 or wider, within the bound.
A program may use at most 128 MiB of HBM per device.

v0:
```python
import jax
import jax.numpy as jnp
from jax import lax
from jax.sharding import PartitionSpec as P

epsilon = 1e-06


def normalize(hidden_state, norm_gain):
    values = hidden_state.astype(jnp.float32)
    inverse_rms = lax.rsqrt(jnp.mean(values * values, axis=-1, keepdims=True) + epsilon)
    return (values * inverse_rms * norm_gain).astype(jnp.bfloat16)


def expert_apply(row_block, gate_matrix, up_matrix, down_matrix):
    gate_part = jnp.dot(row_block, gate_matrix, preferred_element_type=jnp.float32)
    up_part = jnp.dot(row_block, up_matrix, preferred_element_type=jnp.float32)
    activation = (jax.nn.silu(gate_part) * up_part).astype(jnp.bfloat16)
    return jnp.dot(activation, down_matrix, preferred_element_type=jnp.float32)


def on_device(
    hidden_state, norm_gain, expert_ids, gate_logits, gate_weight, up_weight, down_weight
):
    normed = normalize(hidden_state, norm_gain)
    column = lax.all_gather(normed, "rep", axis=0, tiled=True)
    column_rows, top_count = expert_ids.shape
    expert_count = lax.axis_size("ep")
    width = column.shape[1]
    exp_logits = jnp.exp(gate_logits)
    gate_probs = exp_logits / jnp.sum(exp_logits, axis=1, keepdims=True)
    labels = jnp.arange(expert_count, dtype=jnp.int32)
    one_hot = (expert_ids[:, :, None] == labels).astype(jnp.int32)
    hot_rows = column_rows // 2 + 1
    flat_send = one_hot.reshape(column_rows * top_count, expert_count)
    position = jnp.sum((jnp.cumsum(flat_send, axis=0) - flat_send) * flat_send, axis=1)
    valid = jnp.sum(flat_send, axis=1)
    target = jnp.where(valid > 0, expert_ids.reshape(-1) * hot_rows + position, -1)
    slot_labels = jnp.arange(expert_count * hot_rows, dtype=jnp.int32)
    placement_table = (
        (target[:, None] == slot_labels[None, :])
        .astype(jnp.float32)
        .reshape(column_rows, top_count, expert_count * hot_rows)
    )
    dispatch_table = jnp.sum(placement_table, axis=1).astype(jnp.bfloat16)
    combine_table = jnp.sum(placement_table * gate_probs[:, :, None], axis=1)
    outgoing = lax.dot_general(
        dispatch_table, column, (((0,), (0,)), ((), ())), preferred_element_type=jnp.float32
    )
    outgoing = outgoing.astype(jnp.bfloat16).reshape(expert_count, hot_rows, width)
    received = lax.all_to_all(outgoing, "ep", split_axis=0, concat_axis=0, tiled=True)
    block_shape = received.shape
    produced = expert_apply(
        received.reshape(-1, width), gate_weight[0], up_weight[0], down_weight[0]
    ).reshape(block_shape)
    returned = lax.all_to_all(produced, "ep", split_axis=0, concat_axis=0, tiled=True)
    slice_width = returned.shape[2]
    partial_value = jnp.dot(
        combine_table,
        returned.reshape(-1, slice_width),
        precision=lax.Precision.HIGHEST,
        preferred_element_type=jnp.float32,
    )
    return lax.psum_scatter(partial_value, "rep", scatter_dimension=0, tiled=True).astype(
        jnp.bfloat16
    )


def solution(mesh):
    placed = (
        P(("ep", "rep"), None),
        P(),
        P("ep", None),
        P("ep", None),
        P("ep", None, "rep"),
        P("ep", None, "rep"),
        P("ep", "rep", None),
    )
    return jax.shard_map(
        on_device, mesh=mesh, in_specs=placed, out_specs=P(("ep", "rep"), None), check_vma=False
    )
```

profile of v0, /device:TPU:1, one launch (start us, length us, event | category | flops | bytes accessed | tf_op | source)
XLA Modules:
  0.0 1234.6 jit_solution(16467339803064565116)
XLA Ops:
  0.0 0.0 copy-start
  0.0 0.8 copy.22
  0.8 0.1 eq.30
  0.9 0.1 fusion.7
  1.0 0.2 reduce_window_sum.11
  1.2 0.2 select_reduce_fusion.1
  1.4 0.1 gt.15
  1.5 0.1 reduce_sum.58
  1.6 0.7 exponential_reduce_fusion
  2.3 0.7 exponential_divide_fusion
  3.0 0.1 copy.24
  3.1 0.9 fusion.9
  3.9 0.8 fusion.13
  4.8 19.5 %all-gather = bf16[8,2,4096]{2,1,0:T(2,128)(2,1)S(1)} all-gather(bf16[1,2,4096]{2,1,0:T(2,128)(2,1)S(1)} %fusion.13), channel_id=1, replica_groups=mesh['rep'=8,'ep'=64] {'rep'}, dimensions={0}, use_global_device_ids=true | all-gather | bytes 147456 | tf_op jit(solution)/shard_map/all_gather | solution.py:26
  24.2 0.1 reshape.55
  24.3 0.3 convert_reduce_fusion
  24.6 3.6 convolution_convert_fusion
  28.2 8.1 reshape.51
  36.2 375.2 %all_to_all.10 = bf16[64,9,4096]{2,1,0:T(8,128)(2,1)} all-to-all(bf16[64,9,4096]{2,1,0:T(8,128)(2,1)} %reshape.51), channel_id=1, replica_groups=mesh['rep'=8,'ep'=64] {'ep'}, dimensions={0} | all-to-all | bytes 9437184 | tf_op jit(solution)/shard_map/all_to_all | solution.py:51
  411.5 0.0 copy-start.2
  411.5 0.0 copy-start.3
  411.5 8.7 reshape.52
  420.2 0.0 copy-done.2
  420.2 3.7 fusion.4
  423.9 0.0 copy-done.3
  423.9 3.7 fusion
  427.6 0.1 dot_general.20
  427.7 0.0 copy-done
  427.7 5.0 fusion.1
  432.7 15.4 %copy.26 = f32[64,9,4096]{2,1,0:T(8,128)} copy(f32[64,9,4096]{2,0,1:T(8,128)} %fusion.1) | data formatting | bytes 18874368 | tf_op jit(solution)/shard_map/dot_general | solution.py:19
  448.1 14.1 %all-to-all-start.1 = ((f32[64,9,4096]{2,1,0:T(8,128)}), f32[64,9,4096]{2,1,0:T(8,128)}, u32[]{:S(2)}, u32[]{:S(2)}) async-start(f32[64,9,4096]{2,1,0:T(8,128)} %copy.26), calls=%async_computation.1 | async-start | bytes 33554432 | tf_op jit(solution)/shard_map/all_to_all | solution.py:56
  462.2 1.3 dynamic-slice
  464.2 726.0 %all-to-all-done.1 = f32[64,9,4096]{2,1,0:T(8,128)} async-done(((f32[64,9,4096]{2,1,0:T(8,128)}), f32[64,9,4096]{2,1,0:T(8,128)}, u32[]{:S(2)}, u32[]{:S(2)}) %all-to-all-start.1) | async-done | bytes 9437216 | tf_op jit(solution)/shard_map/all_to_all | solution.py:56
  1190.1 0.0 copy-start.1
  1190.1 11.7 reshape.53
  1201.8 7.1 fusion.14
  1208.9 25.0 %all-reduce.2 = bf16[16,4096]{1,0:T(8,128)(2,1)S(1)} all-reduce(f32[16,4096]{1,0:T(8,128)S(1)} %fusion.14), channel_id=2, replica_groups=mesh['rep'=8,'ep'=64] {'rep'}, use_global_device_ids=true, to_apply=%region_7.8.clone | all-reduce | flops 65536 | bytes 393216
  1234.0 0.6 dynamic-slice_convert_fusion
  1234.6 0.0 copy-done.1
  (3 shorter events, 0.0 us)
Async XLA Ops:
  0.0 427.7 %copy-start = (bf16[1,128,4096]{2,1,0:T(8,128)(2,1)S(1)}, bf16[1,128,4096]{2,1,0:T(8,128)(2,1)}, u32[]{:S(2)}) copy-start(bf16[1,128,4096]{2,1,0:T(8,128)(2,1)} %param.13) | copy-start | bytes 3145732
  411.5 8.7 copy-start.2
  411.5 12.4 %copy-start.3 = (bf16[1,4096,128]{2,1,0:T(8,128)(2,1)S(1)}, bf16[1,4096,128]{2,1,0:T(8,128)(2,1)}, u32[]{:S(2)}) copy-start(bf16[1,4096,128]{2,1,0:T(8,128)(2,1)} %param.12) | copy-start | bytes 3145732
  448.1 742.0 %all-to-all-start.1 = ((f32[64,9,4096]{2,1,0:T(8,128)}), f32[64,9,4096]{2,1,0:T(8,128)}, u32[]{:S(2)}, u32[]{:S(2)}) async-start(f32[64,9,4096]{2,1,0:T(8,128)} %copy.26), calls=%async_computation.1 | async-start | bytes 33554432 | tf_op jit(solution)/shard_map/all_to_all | solution.py:56
  1190.1 44.5 %copy-start.1 = (bf16[1,128,4096]{2,1,0:T(8,128)(2,1)S(1)}, bf16[1,128,4096]{2,1,0:T(8,128)(2,1)}, u32[]{:S(2)}) copy-start(bf16[1,128,4096]{2,1,0:T(8,128)(2,1)} %param.13) | copy-start | bytes 3145732
where the time goes:
time: 1240 us; the launch traced here: 1230 us
  waiting for transfers between devices  726 us (59%)
  blocking collectives  420 us (34%)
  local copies, waits for them, and re-layouts  47 us (4%)
  matrix products  23.2 us (2%)
  starting transfers between devices  14.1 us (1%)
    all_to_all x1, waiting for transfers between devices, on_device(): lax.all_to_all(produced, 'ep', split_axis=0, concat_axis=0, tiled=True)  726 us
    all_to_all x1, blocking collectives, on_device(): lax.all_to_all(outgoing, 'ep', split_axis=0, concat_axis=0, tiled=True)  375 us
    unnamed x1, blocking collectives  25 us
  transfers between devices with their start and end apart: 1, of which 1 were waited for; matrix products, arithmetic and copies ran while one was open for 0% of the time, Pallas kernels for 0%

commit v1 on v0

v1 whole, which is shorter than its diff:
```python
import functools

import jax
import jax.numpy as jnp
from jax import lax
from jax.experimental import pallas as pl
from jax.experimental.pallas import tpu as pltpu
from jax.sharding import PartitionSpec as P

epsilon = 1e-06
MESH = pl.DeviceIdType.MESH
Y, C, X, Z = 4, 2, 4, 16
REP = Y * C
COL = 16
TOP = 8
ROWS = X * Z * COL
XROWS = Z * COL
D = 4096
SLICE = D // REP
HALF = SLICE // 2
HID = 128


def kernel(
    hid, gain, tab, gw, uw, dw, out,
    SA, SB, BF, R, T, W, ACC, HF, DT, YF, PB, XR, XS, ZS, ZP, ZR, FA, FB,
    lsem, as_, ar, ds_, dr, zs, zr, ts_, tr, xs, xr, ys, yr, ss, sr,
    txs, txr, hs, hr, hss, hsr, rs, rr, zzs, zzr, fs, fr,
):
    rep = lax.axis_index("rep")
    ep = lax.axis_index("ep")
    y, c = rep // C, lax.rem(rep, C)
    x, z = ep // Z, lax.rem(ep, Z)

    def wrap(v, n):
        return lax.rem(v + n, n)

    def at_rep(r):
        return {"rep": r, "ep": ep}

    def at_ep(e):
        return {"rep": rep, "ep": e}

    xl, xri, xo = wrap(x - 1, X), wrap(x + 1, X), wrap(x + 2, X)
    yl, yri, yo = wrap(y - 1, Y), wrap(y + 1, Y), wrap(y + 2, Y)
    dev_xl, dev_xr = at_ep(xl * Z + z), at_ep(xri * Z + z)
    dev_yl, dev_yr = at_rep(yl * C + c), at_rep(yri * C + c)
    dev_sib = at_rep(y * C + 1 - c)
    zdev = [at_ep(x * Z + lax.rem(z + d, Z)) for d in range(1, Z)]
    rdev = [lax.rem(rep + d, REP) for d in range(1, REP)]

    pending = []

    def send(src, dst, ssem, rsem, dev):
        copy = pltpu.make_async_remote_copy(
            src_ref=src, dst_ref=dst, send_sem=ssem, recv_sem=rsem, device_id=dev, device_id_type=MESH
        )
        copy.start()
        pending.append(copy)
        return copy

    loads = [
        pltpu.make_async_copy(gw.at[0], W.at[:, 0:HID], lsem.at[0]),
        pltpu.make_async_copy(uw.at[0], W.at[:, HID:2 * HID], lsem.at[1]),
    ]
    for load in loads:
        load.start()

    barrier = pltpu.get_barrier_semaphore()
    partners = [at_rep(r) for r in rdev] + [dev_xl, dev_xr] + zdev
    for dev in partners:
        pl.semaphore_signal(barrier, inc=1, device_id=dev, device_id_type=MESH)

    values = hid[...].astype(jnp.float32)
    inverse_rms = lax.rsqrt(jnp.mean(values * values, axis=-1, keepdims=True) + epsilon)
    normed = (values * inverse_rms * gain[...]).astype(jnp.bfloat16)
    for r in range(REP):
        SA[r] = normed[:, r * SLICE:(r + 1) * SLICE]
    row0 = pl.multiple_of(ep * COL, COL)
    xrow0 = pl.multiple_of(x * XROWS, XROWS)
    T[pl.ds(row0, COL), :] = tab[...]
    pl.semaphore_wait(barrier, len(partners))

    first = [
        send(SA.at[r], SB.at[rep], as_.at[i], ar.at[i], at_rep(r)) for i, r in enumerate(rdev)
    ]
    tabs = [
        send(T.at[pl.ds(row0, COL)], T.at[pl.ds(row0, COL)], ts_.at[i], tr.at[i], dev)
        for i, dev in enumerate(zdev)
    ]
    SB[rep] = SA[rep]
    for copy in first:
        copy.wait_recv()
    for r in range(REP):
        BF[2 * r:2 * r + 2, :] = SB[r].astype(jnp.float32)
    block = BF[...].astype(jnp.bfloat16)
    R[y, c, 0, pl.ds(row0, COL), :] = block[:, :HALF]
    R[y, c, 1, pl.ds(row0, COL), :] = block[:, HALF:]
    mine = R.at[y, c, :, pl.ds(row0, COL), :]
    along_z = [send(mine, mine, zs.at[i], zr.at[i], dev) for i, dev in enumerate(zdev)]

    downs = [
        send(
            dw.at[0, :, pl.ds(pl.multiple_of(r * SLICE, SLICE), SLICE)],
            DT.at[rep], ds_.at[i], dr.at[i], at_rep(r),
        )
        for i, r in enumerate(rdev)
    ]
    own_down = pltpu.make_async_copy(
        dw.at[0, :, pl.ds(pl.multiple_of(rep * SLICE, SLICE), SLICE)], DT.at[rep], lsem.at[2]
    )
    own_down.start()
    ACC[...] = jnp.zeros_like(ACC)
    for load in loads:
        load.wait()

    class Ring:
        def __init__(self, view, me, n, left, right, ssem, rsem, base):
            self.view, self.me, self.left, self.right = view, me, left, right
            self.lo, self.hi = wrap(me - 1, n), wrap(me + 1, n)
            self.ssem, self.rsem, self.base = ssem, rsem, base

        def put(self, who, half, dev, k):
            k += self.base
            ref = self.view(who, half)
            return send(ref, ref, self.ssem.at[k], self.rsem.at[k], dev)

        def first(self):
            self.ra = self.put(self.me, 0, self.right, 0)
            self.lb = self.put(self.me, 1, self.left, 1)
            self.rb = self.put(self.me, 1, self.right, 2)
            self.la = self.put(self.me, 0, self.left, 3)

        def relay(self):
            self.ra.wait_recv()
            self.oa = self.put(self.lo, 0, self.right, 4)
            self.lb.wait_recv()
            self.ob = self.put(self.hi, 1, self.left, 5)

        def low(self):
            self.rb.wait_recv()

        def high(self):
            self.la.wait_recv()

        def far(self):
            self.oa.wait_recv()
            self.ob.wait_recv()

    def rows(start, size):
        return pl.ds(pl.multiple_of(start, 16), size)

    ring_t = Ring(
        lambda s, h: T.at[rows(s * XROWS + h * 128, 128), :], x, X, dev_xl, dev_xr, txs, txr, 0
    )
    x1 = Ring(
        lambda s, h: R.at[y, c, 0, rows(s * XROWS + h * 128, 128), :], x, X, dev_xl, dev_xr, xs, xr, 0
    )
    y1 = Ring(
        lambda s, h: R.at[s, c, 1, rows(x * XROWS + h * 128, 128), :], y, Y, dev_yl, dev_yr, ys, yr, 0
    )
    y2 = Ring(
        lambda s, h: R.at[s, c, 0, pl.ds(h * 512, 512), :], y, Y, dev_yl, dev_yr, ys, yr, 6
    )
    x2 = Ring(
        lambda s, h: R.at[pl.ds(2 * h, 2), c, 1, rows(s * XROWS, XROWS), :], x, X, dev_xl, dev_xr, xs, xr, 6
    )

    for copy in along_z:
        copy.wait_recv()
    x1.first()
    y1.first()
    for copy in tabs:
        copy.wait_recv()
    ring_t.first()
    x1.relay()
    y1.relay()
    ring_t.relay()
    x1.low()
    x1.high()
    x1.far()

    def sibling(ref, k):
        return send(ref, ref, ss.at[k], sr.at[k], dev_sib)

    y2.first()
    sib = {}
    sib[0] = sibling(R.at[y, c, 0], 0)
    y1.low()
    y1.high()
    y1.far()
    x2.first()
    sib[1] = sibling(R.at[:, c, 1, rows(x * XROWS, XROWS), :], 1)

    def weight(q):
        return W[pl.ds(pl.multiple_of(q * HALF, HALF), HALF), :]

    def unit_y(yy, cc):
        w = weight((yy * C + cc) * 2)

        def step(i, carry):
            at = rows(i * 256, 256)
            ACC[at, :] += jnp.dot(R[yy, cc, 0, at, :], w, preferred_element_type=jnp.float32)
            return carry

        lax.fori_loop(0, ROWS // 256, step, 0)

    def unit_x(xx, cc):
        at = rows(xx * XROWS, XROWS)

        def step(yy, carry):
            ACC[at, :] += jnp.dot(
                R[yy, cc, 1, at, :], weight((yy * C + cc) * 2 + 1), preferred_element_type=jnp.float32
            )
            return carry

        lax.fori_loop(0, Y, step, 0)

    unit_y(y, c)
    unit_x(x, c)
    sib[0].wait_recv()
    unit_y(y, 1 - c)
    sib[1].wait_recv()
    unit_x(x, 1 - c)
    y2.relay()
    x2.relay()
    y2.low()
    sib[2] = sibling(R.at[yl, c, 0], 2)
    y2.high()
    sib[3] = sibling(R.at[yri, c, 0], 3)
    x2.low()
    sib[4] = sibling(R.at[:, c, 1, rows(xl * XROWS, XROWS), :], 4)
    x2.high()
    sib[5] = sibling(R.at[:, c, 1, rows(xri * XROWS, XROWS), :], 5)
    unit_y(yl, c)
    unit_y(yri, c)
    unit_x(xl, c)
    unit_x(xri, c)
    y2.far()
    sib[6] = sibling(R.at[yo, c, 0], 6)
    x2.far()
    sib[7] = sibling(R.at[:, c, 1, rows(xo * XROWS, XROWS), :], 7)
    unit_y(yo, c)
    unit_x(xo, c)
    for k, (unit, who) in enumerate(
        [(unit_y, yl), (unit_y, yri), (unit_x, xl), (unit_x, xri), (unit_y, yo), (unit_x, xo)]
    ):
        sib[2 + k].wait_recv()
        unit(who, 1 - c)

    def activate(i, carry):
        at = rows(i * 128, 128)
        gate_part = ACC[at, 0:HID]
        up_part = ACC[at, HID:2 * HID]
        HF[y, c, at, :] = (gate_part / (1.0 + jnp.exp(-gate_part)) * up_part).astype(jnp.bfloat16)
        return carry

    lax.fori_loop(0, ROWS // 128, activate, 0)

    def hsib(ref, k):
        return send(ref, ref, hss.at[k], hsr.at[k], dev_sib)

    hring = Ring(lambda s, h: HF.at[s, c, pl.ds(h * 512, 512), :], y, Y, dev_yl, dev_yr, hs, hr, 0)
    hring.first()
    hsibs = [hsib(HF.at[y, c], 0)]
    hring.relay()
    ring_t.low()
    ring_t.high()
    ring_t.far()
    own_down.wait()
    for copy in downs:
        copy.wait_recv()
    hring.low()
    hsibs.append(hsib(HF.at[yl, c], 1))
    hring.high()
    hsibs.append(hsib(HF.at[yri, c], 2))
    hring.far()
    hsibs.append(hsib(HF.at[yo, c], 3))
    for copy in hsibs:
        copy.wait_recv()

    expert = ep.astype(jnp.float32)
    lane = lax.broadcasted_iota(jnp.int32, (XROWS, 128), 1)

    def project(xx):
        at = rows(xx * XROWS, XROWS)
        t = T[at, :].astype(jnp.float32)
        probs = pltpu.roll(t, 128 - TOP, 1) + (pltpu.roll(t, 128 - 2 * TOP, 1) + pltpu.roll(t, 128 - 3 * TOP, 1))
        scale = jnp.sum(jnp.where((lane < TOP) & (t == expert), probs, 0.0), axis=1, keepdims=True)
        total = jnp.zeros((XROWS, SLICE), jnp.float32)
        for yy in range(Y):
            act = jnp.concatenate([HF[yy, 0, at, :], HF[yy, 1, at, :]], axis=1)
            down = DT[2 * yy:2 * yy + 2].reshape(2 * HID, SLICE)
            total += jnp.dot(act, down, preferred_element_type=jnp.float32)
        return total * scale

    def part(xx, keep):
        at = rows(xx * XROWS, XROWS)
        total = project(xx)
        if keep:
            YF[...] = total
        else:
            PB[0, at, :] = total[:, :HALF].astype(jnp.bfloat16)
            PB[1, at, :] = total[:, HALF:].astype(jnp.bfloat16)

    def pb(h, xx):
        return PB.at[h, rows(xx * XROWS, XROWS), :]

    part(xo, False)
    d1 = send(pb(0, xo), XR.at[0], rs.at[0], rr.at[0], dev_xr)
    d2 = send(pb(1, xo), XR.at[1], rs.at[1], rr.at[1], dev_xl)
    part(xri, False)
    d3 = send(pb(1, xri), XR.at[2], rs.at[2], rr.at[2], dev_xr)
    part(xl, False)
    d4 = send(pb(0, xl), XR.at[3], rs.at[3], rr.at[3], dev_xl)
    d1.wait_recv()
    XS[0] = (PB[0, rows(xri * XROWS, XROWS), :].astype(jnp.float32) + XR[0].astype(jnp.float32)).astype(jnp.bfloat16)
    d5 = send(XS.at[0], XR.at[4], rs.at[4], rr.at[4], dev_xr)
    d2.wait_recv()
    XS[1] = (PB[1, rows(xl * XROWS, XROWS), :].astype(jnp.float32) + XR[1].astype(jnp.float32)).astype(jnp.bfloat16)
    d6 = send(XS.at[1], XR.at[5], rs.at[5], rr.at[5], dev_xl)
    part(x, True)
    for copy in (d3, d4, d5, d6):
        copy.wait_recv()
    for h, (one, two) in enumerate(((3, 4), (2, 5))):
        cols = slice(h * HALF, (h + 1) * HALF)
        total = YF[:, cols] + XR[one].astype(jnp.float32) + XR[two].astype(jnp.float32)
        ZS[:, cols] = total
        total = total.astype(jnp.bfloat16)
        for zz in range(Z):
            ZP[zz, :, cols] = total[zz * COL:(zz + 1) * COL]
    back = [
        send(ZP.at[lax.rem(z + d, Z)], ZR.at[d - 1], zzs.at[d - 1], zzr.at[d - 1], zdev[d - 1])
        for d in range(1, Z)
    ]
    for copy in back:
        copy.wait_recv()
    total = ZS[rows(z * COL, COL), :]
    for d in range(1, Z):
        total += ZR[d - 1].astype(jnp.float32)
    total = total.astype(jnp.bfloat16).astype(jnp.float32)
    for r in range(REP):
        FA[r] = total[2 * r:2 * r + 2, :].astype(jnp.bfloat16)
    last = [send(FA.at[r], FB.at[rep], fs.at[i], fr.at[i], at_rep(r)) for i, r in enumerate(rdev)]
    FB[rep] = FA[rep]
    for copy in last:
        copy.wait_recv()
    for r in range(REP):
        out[:, r * SLICE:(r + 1) * SLICE] = FB[r]
    for copy in pending:
        copy.wait_send()


def on_device(
    hidden_state, norm_gain, expert_ids, gate_logits, gate_weight, up_weight, down_weight
):
    exp_logits = jnp.exp(gate_logits)
    gate_probs = exp_logits / jnp.sum(exp_logits, axis=1, keepdims=True)
    hi = lax.reduce_precision(gate_probs, 8, 7)
    mid = lax.reduce_precision(gate_probs - hi, 8, 7)
    low = gate_probs - hi - mid
    table = jnp.concatenate([expert_ids.astype(jnp.float32), hi, mid, low], axis=1)
    table = jnp.pad(table, ((0, 0), (0, 128 - 4 * TOP))).astype(jnp.bfloat16)
    bf, f32 = jnp.bfloat16, jnp.float32
    vmem = pl.BlockSpec(memory_space=pltpu.VMEM)
    hbm = pl.BlockSpec(memory_space=pl.ANY)
    dma = pltpu.SemaphoreType.DMA
    return pl.pallas_call(
        kernel,
        out_shape=jax.ShapeDtypeStruct((COL // REP, D), bf),
        in_specs=[vmem, vmem, vmem, hbm, hbm, hbm],
        out_specs=vmem,
        scratch_shapes=[
            pltpu.VMEM((REP, 2, SLICE), bf),
            pltpu.VMEM((REP, 2, SLICE), bf),
            pltpu.VMEM((COL, SLICE), f32),
            pltpu.VMEM((Y, C, 2, ROWS, HALF), bf),
            pltpu.VMEM((ROWS, 128), bf),
            pltpu.VMEM((D, 2 * HID), bf),
            pltpu.VMEM((ROWS, 2 * HID), f32),
            pltpu.VMEM((Y, C, ROWS, HID), bf),
            pltpu.VMEM((REP, HID, SLICE), bf),
            pltpu.VMEM((XROWS, SLICE), f32),
            pltpu.VMEM((2, ROWS, HALF), bf),
            pltpu.VMEM((6, XROWS, HALF), bf),
            pltpu.VMEM((2, XROWS, HALF), bf),
            pltpu.VMEM((XROWS, SLICE), f32),
            pltpu.VMEM((Z, COL, SLICE), bf),
            pltpu.VMEM((Z - 1, COL, SLICE), bf),
            pltpu.VMEM((REP, 2, SLICE), bf),
            pltpu.VMEM((REP, 2, SLICE), bf),
            dma((3,)),
            dma((REP - 1,)), dma((REP - 1,)),
            dma((REP - 1,)), dma((REP - 1,)),
            dma((Z - 1,)), dma((Z - 1,)),
            dma((Z - 1,)), dma((Z - 1,)),
            dma((12,)), dma((12,)),
            dma((12,)), dma((12,)),
            dma((8,)), dma((8,)),
            dma((6,)), dma((6,)),
            dma((6,)), dma((6,)),
            dma((4,)), dma((4,)),
            dma((6,)), dma((6,)),
            dma((Z - 1,)), dma((Z - 1,)),
            dma((REP - 1,)), dma((REP - 1,)),
        ],
        compiler_params=pltpu.CompilerParams(
            collective_id=0, has_side_effects=True, vmem_limit_bytes=56 * 1024 * 1024
        ),
    )(hidden_state, norm_gain.reshape(1, D), table, gate_weight, up_weight, down_weight)


def solution(mesh):
    placed = (
        P(("ep", "rep"), None),
        P(),
        P("ep", None),
        P("ep", None),
        P("ep", None, "rep"),
        P("ep", None, "rep"),
        P("ep", "rep", None),
    )
    return jax.shard_map(
        on_device, mesh=mesh, in_specs=placed, out_specs=P(("ep", "rep"), None), check_vma=False
    )
```

time: 1240 us -> 117 us (0.09)
  waiting for transfers between devices: 726 us -> 0 us
  blocking collectives: 420 us -> 0 us
  Pallas kernels: 0 us -> 113 us
  local copies, waits for them, and re-layouts: 47 us -> 2.09 us
  matrix products: 23.2 us -> 0 us
  starting transfers between devices: 14.1 us -> 0 us
    all_to_all x1 -> x0, waiting for transfers between devices: 726 us -> none  [on_device(): lax.all_to_all(produced, 'ep', split_axis=0, concat_axis=0, tiled=True)]
    all_to_all x1 -> x0, blocking collectives: 375 us -> none  [on_device(): lax.all_to_all(outgoing, 'ep', split_axis=0, concat_axis=0, tiled=True)]
    pallas_call x0 -> x1, Pallas kernels: none -> 113 us  [on_device(): pl.pallas_call(kernel, out_shape=jax.ShapeDtypeStruct((COL // REP, D), bf...]
    reshape x3 -> x0, local copies, waits for them, and re-layouts: 28.4 us -> none  [the longest x1 11.7 us: on_device(): returned.reshape(-1, slice_width)]
    unnamed x1 -> x0, blocking collectives: 25 us -> none
    dot_general x5 -> x0, matrix products: 23.2 us -> none  [the longest x1 7.14 us: on_device(): jnp.dot(combine_table, returned.reshape(-1, slice_width), precision=lax.P...]
    all_gather x1 -> x0, blocking collectives: 19.5 us -> none  [on_device(): column = lax.all_gather(normed, 'rep', axis=0, tiled=True)]
    dot_general x2 -> x0, local copies, waits for them, and re-layouts: 15.5 us -> none  [expert_apply(): return jnp.dot(activation, down_matrix, preferred_element_type=jnp.float32)]
  transfers between devices with their start and end apart: 1 -> 0, of which waited for: 1 -> 0; matrix products, arithmetic and copies ran while one was open for 0% -> 0% of each run, Pallas kernels for 0% -> 0%
where the time goes in v1:
time: 117 us; the launch traced here: 116 us
  Pallas kernels  113 us (97%)
  local copies, waits for them, and re-layouts  2.09 us (2%)
  other arithmetic  1.47 us (1%)
    pallas_call x1, Pallas kernels, on_device(): pl.pallas_call(kernel, out_shape=jax.ShapeDtypeStruct((COL // REP, D), bf...  113 us

profile of v1, /device:TPU:1, one launch (start us, length us, event | category | flops | bytes accessed | tf_op | source)
XLA Modules:
  0.0 116.4 jit_solution(3675694957392747320)
XLA Ops:
  0.0 0.7 convert_element_type.6
  0.7 0.0 copy-start
  0.7 0.1 copy.10
  0.8 0.6 copy-done
  1.4 0.1 copy.11
  1.5 0.1 reduce-precision_convert_fusion.1
  1.6 0.7 fusion.7.tab
  2.2 112.8 %shard_map.73 = bf16[2,4096]{1,0:T(2,128)(2,1)} custom-call(bf16[2,4096]{1,0:T(2,128)(2,1)} %hid.1, f32[1,4096]{1,0:T(1,128)} %bitcast.1, bf16[16,128]{1,0:T(8,128)(2,1)} %fusion.7.tab, bf16[1,4096,128]{2,1,0:T(8,128)(2,1)} %gw.1, bf16[1,4096,128]{2,1,0:T(8,128)(2,1)} %uw.1, bf16[1,128,4096]{2,1,0:T(8,128)(2,1)} %dw.1), custom_call_target="tpu_custom_call" | custom-call | tf_op jit(solution)/shard_map/pallas_call | solution.py:368
  115.1 1.3 %copy.13 = bf16[2,4096]{1,0:T(2,128)(2,1)} copy(bf16[2,4096]{1,0:T(2,128)(2,1)} %shard_map.73) | data formatting | bytes 32768
  (1 shorter events, 0.0 us)
Async XLA Ops:
  0.7 0.7 copy-start

commit v2 on v0

v2 whole, which is shorter than its diff:
```python
import jax
import jax.numpy as jnp
from jax import lax
from jax.experimental import pallas as pl
from jax.experimental.pallas import tpu as pltpu
from jax.sharding import PartitionSpec as P

epsilon = 1e-06
MESH = pl.DeviceIdType.MESH
Y, C, X, Z = 4, 2, 4, 16
ZQ = 4
REP = Y * C
COL = 16
TOP = 8
ROWS = X * Z * COL
XROWS = Z * COL
D = 4096
SLICE = D // REP
HALF = SLICE // 2
HID = 128
SENDS = 240


def kernel(
    hid, gain, ids, logits, gw, uw, dw, out,
    SA, SB, BF, TB, R, T, W, ACC, HF, DT, PB, ZA, ZB, FA, FB,
    lsem, ssem, rsem,
):
    rep = lax.axis_index("rep")
    ep = lax.axis_index("ep")
    y, c = rep // C, lax.rem(rep, C)
    x, z = ep // Z, lax.rem(ep, Z)
    zhi, zlo = z // ZQ, lax.rem(z, ZQ)
    f32, bf16 = jnp.float32, jnp.bfloat16

    def wrap(v, n):
        return lax.rem(v + n, n)

    def at_rep(r):
        return {"rep": r, "ep": ep}

    def at_ep(e):
        return {"rep": rep, "ep": e}

    def at_z(d):
        return at_ep(x * Z + wrap(z + d, Z))

    xl, xri, xo = wrap(x - 1, X), wrap(x + 1, X), wrap(x + 2, X)
    yl, yri, yo = wrap(y - 1, Y), wrap(y + 1, Y), wrap(y + 2, Y)
    dev_x = (at_ep(xl * Z + z), at_ep(xri * Z + z))
    dev_y = (at_rep(yl * C + c), at_rep(yri * C + c))
    dev_sib = at_rep(y * C + 1 - c)
    rdev = [lax.rem(rep + d, REP) for d in range(1, REP)]

    pending = []

    def send(src, dst, dev):
        k = len(pending)
        copy = pltpu.make_async_remote_copy(
            src_ref=src, dst_ref=dst, send_sem=ssem.at[k], recv_sem=rsem.at[k], device_id=dev, device_id_type=MESH
        )
        copy.start()
        pending.append(copy)
        return copy

    def share(ref, dev):
        return send(ref, ref, dev)

    barrier = pltpu.get_barrier_semaphore()
    def at_class(k, r):
        return {"rep": r, "ep": x * Z + wrap(zhi + k, ZQ) * ZQ + zlo}

    spread = [(k, at_class(k, lax.rem(rep + d, REP)), d) for k in range(ZQ) for d in range(REP) if k or d]
    def at_xz(xx, d):
        return at_ep(xx * Z + wrap(z + d, Z))

    partners = [dev for _, dev, _ in spread]
    partners += [at_xz(xx, d) for xx in (xl, xri, xo) for d in (0, 1, -1, 2, -2)]
    partners += [at_z(d) for d in (1, -1, 2, -2)]
    for dev in partners:
        pl.semaphore_signal(barrier, inc=1, device_id=dev, device_id_type=MESH)
    loads = [
        pltpu.make_async_copy(gw.at[0], W.at[:, 0:HID], lsem.at[0]),
        pltpu.make_async_copy(uw.at[0], W.at[:, HID:2 * HID], lsem.at[1]),
    ]
    for load in loads:
        load.start()

    values = hid[...].astype(f32)
    inverse_rms = lax.rsqrt(jnp.mean(values * values, axis=-1, keepdims=True) + epsilon)
    normed = (values * inverse_rms * gain[...]).astype(bf16)
    for r in range(REP):
        SA[r] = normed[:, r * SLICE:(r + 1) * SLICE]
    exp_logits = jnp.exp(logits[...])
    probs = exp_logits / jnp.sum(exp_logits, axis=1, keepdims=True)
    high = probs.astype(bf16).astype(f32)
    middle = (probs - high).astype(bf16).astype(f32)
    TB[...] = jnp.zeros_like(TB)
    TB[:, 0:TOP] = ids[...].astype(f32)
    TB[:, TOP:2 * TOP] = high
    TB[:, 2 * TOP:3 * TOP] = middle
    TB[:, 3 * TOP:4 * TOP] = probs - high - middle
    T[x, zhi, zlo] = TB[...].astype(bf16)
    pl.semaphore_wait(barrier, len(partners))

    first = [send(SA.at[lax.rem(rep + d, REP)], SB.at[zhi, rep], dev) for _, dev, d in spread]
    tlevel = [share(T.at[x, zhi, zlo], at_class(k, rep)) for k in range(1, ZQ)]
    def down_slice(r):
        return dw.at[0, :, pl.ds(pl.multiple_of(r * SLICE, SLICE), SLICE)]

    downs = [send(down_slice(r), DT.at[rep], at_rep(r)) for r in rdev]
    own_down = pltpu.make_async_copy(down_slice(rep), DT.at[rep], lsem.at[2])
    own_down.start()
    SB[zhi, rep] = SA[rep]
    for copy in first:
        copy.wait_recv()
    q0 = rep * 2
    for k in range(ZQ):
        for r in range(REP):
            BF[k, 2 * r:2 * r + 2, :] = SB[k, r].astype(f32)
    for k in range(ZQ):
        block = BF[k].astype(bf16)
        R[q0, x, k, zlo] = block[:, :HALF]
        R[q0 + 1, x, k, zlo] = block[:, HALF:]
    both = R.at[pl.ds(q0, 2), x, :, zlo]
    level = [share(both, at_z(1)), share(both, at_z(-1))]
    level += [share(R.at[q0, x, :, zlo], at_z(2)), share(R.at[q0 + 1, x, :, zlo], at_z(-2))]
    for copy in tlevel:
        copy.wait_recv()
    tlevel = [share(T.at[x, :, zlo], at_z(d)) for d in (1, -1, 2)]

    class Ring:
        def __init__(self, view, me, n, devs):
            self.view, self.me, self.devs = view, me, devs
            self.lo, self.hi = wrap(me - 1, n), wrap(me + 1, n)

        def put(self, who, half, side):
            return share(self.view(who, half), self.devs[side])

        def first(self):
            self.ra = self.put(self.me, 0, 1)
            self.lb = self.put(self.me, 1, 0)
            self.rb = self.put(self.me, 1, 1)
            self.la = self.put(self.me, 0, 0)
            return self

        def relay(self):
            self.ra.wait_recv()
            self.oa = self.put(self.lo, 0, 1)
            self.lb.wait_recv()
            self.ob = self.put(self.hi, 1, 0)

        def low(self):
            self.rb.wait_recv()

        def high(self):
            self.la.wait_recv()

        def far(self):
            self.oa.wait_recv()
            self.ob.wait_recv()

    def piece(yy, h, xx):
        return R.at[(yy * C + c) * 2 + h, xx]

    def cut(ref, half):
        return ref.at[pl.ds(2 * half, 2)]

    def along_y(h, xx):
        return Ring(lambda s, half: cut(piece(s, h, xx), half), y, Y, dev_y)

    def along_x(h, yy):
        return Ring(lambda s, half: cut(piece(yy, h, s), half), x, X, dev_x)

    sib = {}

    def forward(yy, h, xx, name):
        sib[name + (h,)] = share(piece(yy, h, xx), dev_sib)

    for load in loads:
        load.wait()
    for copy in level:
        copy.wait_recv()
    x1 = along_x(0, y).first()
    y1 = along_y(1, x).first()
    y2 = {"own": along_y(0, x).first()}
    x2 = {"own": along_x(1, y).first()}
    for copy in tlevel:
        copy.wait_recv()
    ring_t = Ring(lambda s, h: T.at[s, pl.ds(2 * h, 2)], x, X, dev_x).first()
    forward(y, 0, x, ("own", "own"))
    forward(y, 1, x, ("own", "own"))
    x1.relay()
    y1.relay()
    x1.low()
    y2["low"] = along_y(0, xl).first()
    y1.low()
    x2["low"] = along_x(1, yl).first()
    x1.high()
    y2["high"] = along_y(0, xri).first()
    y1.high()
    x2["high"] = along_x(1, yri).first()
    forward(y, 0, xl, ("own", "low"))
    forward(y, 0, xri, ("own", "high"))
    forward(yl, 1, x, ("low", "own"))
    forward(yri, 1, x, ("high", "own"))
    y2["own"].relay()
    x2["own"].relay()
    x1.far()
    y2["far"] = along_y(0, xo).first()
    y1.far()
    x2["far"] = along_x(1, yo).first()
    forward(y, 0, xo, ("own", "far"))
    forward(yo, 1, x, ("far", "own"))
    xname = {"own": x, "low": xl, "high": xri, "far": xo}
    yname = {"own": y, "low": yl, "high": yri, "far": yo}

    def near_y(g):
        y2[g].low()
        forward(yl, 0, xname[g], ("low", g))
        y2[g].high()
        forward(yri, 0, xname[g], ("high", g))

    def far_y(g):
        y2[g].far()
        forward(yo, 0, xname[g], ("far", g))

    def near_x(g):
        x2[g].low()
        forward(yname[g], 1, xl, (g, "low"))
        x2[g].high()
        forward(yname[g], 1, xri, (g, "high"))

    def far_x(g):
        x2[g].far()
        forward(yname[g], 1, xo, (g, "far"))

    def gathered(g):
        for name in list(sib):
            if name[1] == g:
                sib.pop(name).wait_recv()

    def gateup(xx):
        total = None
        for q in range(2 * REP):
            part = jnp.dot(
                R[q, xx].reshape(XROWS, HALF), W[q * HALF:(q + 1) * HALF, :], preferred_element_type=f32
            )
            total = part if total is None else total + part
        ACC[...] = total
        for i in range(2):
            at = slice(i * 128, (i + 1) * 128)
            gate_part = ACC[at, 0:HID]
            up_part = ACC[at, HID:2 * HID]
            HF[y, c, xx, at, :] = (gate_part / (1.0 + jnp.exp(-gate_part)) * up_part).astype(bf16)

    hrings = {}
    hsibs = {}

    def hstart(g):
        xx = xname[g]
        hrings[g] = Ring(lambda s, half: HF.at[s, c, xx, pl.ds(half * 128, 128)], y, Y, dev_y).first()
        hsibs[g] = [share(HF.at[y, c, xx], dev_sib)]

    def hnear(g):
        xx = xname[g]
        hrings[g].relay()
        hrings[g].low()
        hsibs[g].append(share(HF.at[yl, c, xx], dev_sib))
        hrings[g].high()
        hsibs[g].append(share(HF.at[yri, c, xx], dev_sib))

    def hfar(g):
        hrings[g].far()
        hsibs[g].append(share(HF.at[yo, c, xname[g]], dev_sib))

    def hdone(g):
        for copy in hsibs[g]:
            copy.wait_recv()

    near_y("own")
    near_x("own")
    y2["low"].relay()
    x2["low"].relay()
    y2["high"].relay()
    x2["high"].relay()
    far_y("own")
    far_x("own")
    gathered("own")
    gateup(x)
    hstart("own")
    near_y("low")
    near_x("low")
    near_y("high")
    near_x("high")
    y2["far"].relay()
    x2["far"].relay()
    far_y("low")
    far_x("low")
    far_y("high")
    far_x("high")
    hnear("own")
    near_y("far")
    near_x("far")
    gathered("low")
    gateup(xl)
    hstart("low")
    gathered("high")
    gateup(xri)
    hstart("high")
    far_y("far")
    far_x("far")
    ring_t.relay()
    hfar("own")
    hnear("low")
    hnear("high")
    gathered("far")
    gateup(xo)
    hlast = [share(HF.at[y, c, xo], at_rep(to * C + c)) for to in (yl, yri, yo)]
    hsibs["far"] = [share(HF.at[y, c, xo], dev_sib)]
    ring_t.low()
    ring_t.high()
    ring_t.far()
    own_down.wait()
    for copy in downs:
        copy.wait_recv()

    expert = ep.astype(f32)
    lane = lax.broadcasted_iota(jnp.int32, (XROWS, 128), 1)

    def project(xx):
        t = T[xx].reshape(XROWS, 128).astype(f32)
        parts = pltpu.roll(t, 128 - TOP, 1) + (pltpu.roll(t, 128 - 2 * TOP, 1) + pltpu.roll(t, 128 - 3 * TOP, 1))
        scale = jnp.sum(jnp.where((lane < TOP) & (t == expert), parts, 0.0), axis=1, keepdims=True)
        total = jnp.zeros((XROWS, SLICE), f32)
        for yy in range(Y):
            act = jnp.concatenate([HF[yy, 0, xx], HF[yy, 1, xx]], axis=1)
            down = DT[2 * yy:2 * yy + 2].reshape(2 * HID, SLICE)
            total += jnp.dot(act, down, preferred_element_type=f32)
        return total * scale

    def part(xx):
        total = project(xx).astype(bf16)
        for h in range(2):
            for zz in range(Z):
                PB[xx, h, zz % ZQ, zz // ZQ] = total[zz * COL:(zz + 1) * COL, h * HALF:(h + 1) * HALF]

    scattered = []

    def scatter(xx, own):
        if own:
            ZA[x, 0] = PB[x, :, zlo]
        else:
            scattered.append(send(PB.at[xx, :, zlo], ZA.at[x, 0], at_xz(xx, 0)))
        for k, d in ((1, 1), (2, -1)):
            scattered.append(send(PB.at[xx, :, wrap(zlo + d, ZQ)], ZA.at[x, k], at_xz(xx, d)))
        for k, d in ((0, 2), (1, -2)):
            scattered.append(send(PB.at[xx, k, wrap(zlo + 2, ZQ)], ZB.at[x, k], at_xz(xx, d)))

    hfar("low")
    hfar("high")
    hdone("low")
    part(xl)
    scatter(xl, False)
    hdone("high")
    part(xri)
    scatter(xri, False)
    hdone("own")
    part(x)
    scatter(x, True)
    for copy, who in zip(hlast, (yri, yl, yo)):
        copy.wait_recv()
        hsibs["far"].append(share(HF.at[who, c, xo], dev_sib))
    hdone("far")
    part(xo)
    scatter(xo, False)
    for copy in scattered:
        copy.wait_recv()
    for h in range(2):
        total = jnp.zeros((ZQ, COL, HALF), f32)
        for xx in range(X):
            for k in range(3):
                total += ZA[xx, k, h].astype(f32)
            total += ZB[xx, h].astype(f32)
        for k in range(ZQ):
            BF[k, :, h * HALF:(h + 1) * HALF] = total[k]
    for k in range(ZQ):
        for r in range(REP):
            FA[k, r] = BF[k, 2 * r:2 * r + 2, :].astype(bf16)
    last = [
        send(FA.at[wrap(zhi + k, ZQ), lax.rem(rep + d, REP)], FB.at[zhi, rep], dev) for k, dev, d in spread
    ]
    FB[zhi, rep] = FA[zhi, rep]
    for copy in last:
        copy.wait_recv()
    for r in range(REP):
        total = FB[0, r].astype(f32)
        for k in range(1, ZQ):
            total += FB[k, r].astype(f32)
        out[:, r * SLICE:(r + 1) * SLICE] = total.astype(bf16)
    for copy in pending:
        copy.wait_send()


def on_device(
    hidden_state, norm_gain, expert_ids, gate_logits, gate_weight, up_weight, down_weight
):
    bf, f32 = jnp.bfloat16, jnp.float32
    vmem = pl.BlockSpec(memory_space=pltpu.VMEM)
    hbm = pl.BlockSpec(memory_space=pl.ANY)
    dma = pltpu.SemaphoreType.DMA
    return pl.pallas_call(
        kernel,
        out_shape=jax.ShapeDtypeStruct((COL // REP, D), bf),
        in_specs=[vmem, vmem, vmem, vmem, hbm, hbm, hbm],
        out_specs=vmem,
        scratch_shapes=[
            pltpu.VMEM((REP, 2, SLICE), bf),
            pltpu.VMEM((ZQ, REP, 2, SLICE), bf),
            pltpu.VMEM((ZQ, COL, SLICE), f32),
            pltpu.VMEM((COL, 128), f32),
            pltpu.VMEM((2 * REP, X, ZQ, ZQ, COL, HALF), bf),
            pltpu.VMEM((X, ZQ, ZQ, COL, 128), bf),
            pltpu.VMEM((D, 2 * HID), bf),
            pltpu.VMEM((XROWS, 2 * HID), f32),
            pltpu.VMEM((Y, C, X, XROWS, HID), bf),
            pltpu.VMEM((REP, HID, SLICE), bf),
            pltpu.VMEM((X, 2, ZQ, ZQ, COL, HALF), bf),
            pltpu.VMEM((X, 3, 2, ZQ, COL, HALF), bf),
            pltpu.VMEM((X, 2, ZQ, COL, HALF), bf),
            pltpu.VMEM((ZQ, REP, 2, SLICE), bf),
            pltpu.VMEM((ZQ, REP, 2, SLICE), bf),
            dma((3,)),
            dma((SENDS,)),
            dma((SENDS,)),
        ],
        compiler_params=pltpu.CompilerParams(
            collective_id=0, has_side_effects=True, vmem_limit_bytes=56 * 1024 * 1024
        ),
    )(hidden_state, norm_gain.reshape(1, D), expert_ids, gate_logits, gate_weight, up_weight, down_weight)


def solution(mesh):
    placed = (
        P(("ep", "rep"), None),
        P(),
        P("ep", None),
        P("ep", None),
        P("ep", None, "rep"),
        P("ep", None, "rep"),
        P("ep", "rep", None),
    )
    return jax.shard_map(
        on_device, mesh=mesh, in_specs=placed, out_specs=P(("ep", "rep"), None), check_vma=False
    )
```

time: 1240 us -> 104 us (0.08)
  waiting for transfers between devices: 726 us -> 0 us
  blocking collectives: 420 us -> 0 us
  Pallas kernels: 0 us -> 101 us
  local copies, waits for them, and re-layouts: 47 us -> 3.37 us
  matrix products: 23.2 us -> 0 us
  starting transfers between devices: 14.1 us -> 0 us
    all_to_all x1 -> x0, waiting for transfers between devices: 726 us -> none  [on_device(): lax.all_to_all(produced, 'ep', split_axis=0, concat_axis=0, tiled=True)]
    all_to_all x1 -> x0, blocking collectives: 375 us -> none  [on_device(): lax.all_to_all(outgoing, 'ep', split_axis=0, concat_axis=0, tiled=True)]
    pallas_call x0 -> x1, Pallas kernels: none -> 101 us  [on_device(): pl.pallas_call(kernel, out_shape=jax.ShapeDtypeStruct((COL // REP, D), bf...]
    reshape x3 -> x0, local copies, waits for them, and re-layouts: 28.4 us -> none  [the longest x1 11.7 us: on_device(): returned.reshape(-1, slice_width)]
    unnamed x1 -> x0, blocking collectives: 25 us -> none
    dot_general x5 -> x0, matrix products: 23.2 us -> none  [the longest x1 7.14 us: on_device(): jnp.dot(combine_table, returned.reshape(-1, slice_width), precision=lax.P...]
    all_gather x1 -> x0, blocking collectives: 19.5 us -> none  [on_device(): column = lax.all_gather(normed, 'rep', axis=0, tiled=True)]
    dot_general x2 -> x0, local copies, waits for them, and re-layouts: 15.5 us -> none  [expert_apply(): return jnp.dot(activation, down_matrix, preferred_element_type=jnp.float32)]
  transfers between devices with their start and end apart: 1 -> 0, of which waited for: 1 -> 0; matrix products, arithmetic and copies ran while one was open for 0% -> 0% of each run, Pallas kernels for 0% -> 0%
where the time goes in v2:
time: 104 us
  Pallas kernels  101 us (97%)
  local copies, waits for them, and re-layouts  3.37 us (3%)
    pallas_call x1, Pallas kernels, on_device(): pl.pallas_call(kernel, out_shape=jax.ShapeDtypeStruct((COL // REP, D), bf...  101 us
    unnamed x5, local copies, waits for them, and re-layouts  3.37 us

profile of v2, /device:TPU:1, one launch (start us, length us, event | category | flops | bytes accessed | tf_op | source)
XLA Modules:
  0.0 104.1 jit_solution(5101604494579164031)
XLA Ops:
  0.0 0.0 copy-start
  0.0 1.4 %copy.8.ids = s32[16,8]{1,0:T(8,128)} copy(s32[16,8]{0,1:T(8,128)} %param.9) | data formatting | bytes 1024 | tf_op args[2]
  1.4 0.0 copy-done
  1.4 0.7 copy.9.logits
  2.0 100.7 %shard_map.73 = bf16[2,4096]{1,0:T(2,128)(2,1)} custom-call(bf16[2,4096]{1,0:T(2,128)(2,1)} %hid.1, f32[1,4096]{1,0:T(1,128)} %bitcast.1, s32[16,8]{1,0:T(8,128)} %copy.8.ids, f32[16,8]{1,0:T(8,128)} %copy.9.logits, bf16[1,4096,128]{2,1,0:T(8,128)(2,1)} %gw.1, bf16[1,4096,128]{2,1,0:T(8,128)(2,1)} %uw.1, bf16[1,128,4096]{2,1,0:T(8,128)(2,1)} %dw.1), custom_call_target="tpu_custom_call" | custom-call | tf_op jit(solution)/shard_map/pallas_call | solution.py:412
  102.8 1.3 %copy.11 = bf16[2,4096]{1,0:T(2,128)(2,1)} copy(bf16[2,4096]{1,0:T(2,128)(2,1)} %shard_map.73) | data formatting | bytes 32768
Async XLA Ops:
  0.0 1.4 %copy-start = (f32[16,8]{0,1:T(8,128)S(1)}, f32[16,8]{0,1:T(8,128)}, u32[]{:S(2)}) copy-start(f32[16,8]{0,1:T(8,128)} %param.10) | copy-start | bytes 1540

commit v3 on v2

--- a/solution.py
+++ b/solution.py
@@ -23,7 +23,7 @@
 
 def kernel(
     hid, gain, ids, logits, gw, uw, dw, out,
-    SA, SB, BF, TB, R, T, W, ACC, HF, DT, PB, ZA, ZB, FA, FB,
+    SA, SB, BF, R, T, W, ACC, HF, DT, PB, ZA, ZB, FA, FB,
     lsem, ssem, rsem,
 ):
     rep = lax.axis_index("rep")
@@ -92,15 +92,15 @@
     for r in range(REP):
         SA[r] = normed[:, r * SLICE:(r + 1) * SLICE]
     exp_logits = jnp.exp(logits[...])
-    probs = exp_logits / jnp.sum(exp_logits, axis=1, keepdims=True)
+    probs = exp_logits / jnp.sum(exp_logits, axis=0, keepdims=True)
     high = probs.astype(bf16).astype(f32)
     middle = (probs - high).astype(bf16).astype(f32)
-    TB[...] = jnp.zeros_like(TB)
-    TB[:, 0:TOP] = ids[...].astype(f32)
-    TB[:, TOP:2 * TOP] = high
-    TB[:, 2 * TOP:3 * TOP] = middle
-    TB[:, 3 * TOP:4 * TOP] = probs - high - middle
-    T[x, zhi, zlo] = TB[...].astype(bf16)
+    stacked = jnp.concatenate([ids[...].astype(f32), high, middle, probs - high - middle], axis=0)
+    shape = (4 * TOP, 128)
+    pick = lax.broadcasted_iota(jnp.int32, shape, 0) == lax.broadcasted_iota(jnp.int32, shape, 1)
+    T[x, zhi, zlo] = lax.dot_general(
+        stacked.astype(bf16), pick.astype(f32).astype(bf16), (((0,), (0,)), ((), ())), preferred_element_type=f32
+    ).astype(bf16)
     pl.semaphore_wait(barrier, len(partners))
 
     first = [send(SA.at[lax.rem(rep + d, REP)], SB.at[zhi, rep], dev) for _, dev, d in spread]
@@ -185,9 +185,6 @@
     y1 = along_y(1, x).first()
     y2 = {"own": along_y(0, x).first()}
     x2 = {"own": along_x(1, y).first()}
-    for copy in tlevel:
-        copy.wait_recv()
-    ring_t = Ring(lambda s, h: T.at[s, pl.ds(2 * h, 2)], x, X, dev_x).first()
     forward(y, 0, x, ("own", "own"))
     forward(y, 1, x, ("own", "own"))
     x1.relay()
@@ -278,6 +275,9 @@
         for copy in hsibs[g]:
             copy.wait_recv()
 
+    for copy in tlevel:
+        copy.wait_recv()
+    ring_t = Ring(lambda s, h: T.at[s, pl.ds(2 * h, 2)], x, X, dev_x).first()
     near_y("own")
     near_x("own")
     y2["low"].relay()
@@ -316,7 +316,7 @@
     hnear("high")
     gathered("far")
     gateup(xo)
-    hlast = [share(HF.at[y, c, xo], at_rep(to * C + c)) for to in (yl, yri, yo)]
+    hlast = [share(HF.at[y, c, xo], at_rep(to * C + c)) for to in (yo, yl, yri)]
     hsibs["far"] = [share(HF.at[y, c, xo], dev_sib)]
     ring_t.low()
     ring_t.high()
@@ -368,7 +368,7 @@
     hdone("own")
     part(x)
     scatter(x, True)
-    for copy, who in zip(hlast, (yri, yl, yo)):
+    for copy, who in zip(hlast[1:] + hlast[:1], (yri, yl, yo)):
         copy.wait_recv()
         hsibs["far"].append(share(HF.at[who, c, xo], dev_sib))
     hdone("far")
@@ -391,6 +391,8 @@
         send(FA.at[wrap(zhi + k, ZQ), lax.rem(rep + d, REP)], FB.at[zhi, rep], dev) for k, dev, d in spread
     ]
     FB[zhi, rep] = FA[zhi, rep]
+    for copy in pending[:-len(last)]:
+        copy.wait_send()
     for copy in last:
         copy.wait_recv()
     for r in range(REP):
@@ -398,7 +400,7 @@
         for k in range(1, ZQ):
             total += FB[k, r].astype(f32)
         out[:, r * SLICE:(r + 1) * SLICE] = total.astype(bf16)
-    for copy in pending:
+    for copy in last:
         copy.wait_send()
 
 
@@ -418,7 +420,6 @@
             pltpu.VMEM((REP, 2, SLICE), bf),
             pltpu.VMEM((ZQ, REP, 2, SLICE), bf),
             pltpu.VMEM((ZQ, COL, SLICE), f32),
-            pltpu.VMEM((COL, 128), f32),
             pltpu.VMEM((2 * REP, X, ZQ, ZQ, COL, HALF), bf),
             pltpu.VMEM((X, ZQ, ZQ, COL, 128), bf),
             pltpu.VMEM((D, 2 * HID), bf),
@@ -437,7 +438,7 @@
         compiler_params=pltpu.CompilerParams(
             collective_id=0, has_side_effects=True, vmem_limit_bytes=56 * 1024 * 1024
         ),
-    )(hidden_state, norm_gain.reshape(1, D), expert_ids, gate_logits, gate_weight, up_weight, down_weight)
+    )(hidden_state, norm_gain.reshape(1, D), expert_ids.T, gate_logits.T, gate_weight, up_weight, down_weight)
 
 
 def solution(mesh):

time: 104 us -> 102 us (0.981)
  local copies, waits for them, and re-layouts: 3.37 us -> 1.34 us
    unnamed x5 -> x1, local copies, waits for them, and re-layouts: 3.37 us -> 1.34 us
where the time goes in v3:
time: 102 us
  Pallas kernels  100 us (98%)
  local copies, waits for them, and re-layouts  1.34 us (1%)
    pallas_call x1, Pallas kernels, on_device(): pl.pallas_call(kernel, out_shape=jax.ShapeDtypeStruct((COL // REP, D), bf...  100 us

profile of v3, /device:TPU:1, one launch (start us, length us, event | category | flops | bytes accessed | tf_op | source)
XLA Modules:
  0.0 101.6 jit_solution(12725097617714804371)
XLA Ops:
  0.0 100.2 %shard_map.73 = bf16[2,4096]{1,0:T(2,128)(2,1)} custom-call(bf16[2,4096]{1,0:T(2,128)(2,1)} %hid.1, f32[1,4096]{1,0:T(1,128)} %bitcast.3, s32[8,16]{1,0:T(8,128)} %bitcast.4, f32[8,16]{1,0:T(8,128)} %bitcast.5, bf16[1,4096,128]{2,1,0:T(8,128)(2,1)} %gw.1, bf16[1,4096,128]{2,1,0:T(8,128)(2,1)} %uw.1, bf16[1,128,4096]{2,1,0:T(8,128)(2,1)} %dw.1), custom_call_target="tpu_custom_call" | custom-call | tf_op jit(solution)/shard_map/pallas_call | solution.py:414
  100.2 1.3 %copy.9 = bf16[2,4096]{1,0:T(2,128)(2,1)} copy(bf16[2,4096]{1,0:T(2,128)(2,1)} %shard_map.73) | data formatting | bytes 32768

commit v4 on v3

--- a/solution.py
+++ b/solution.py
@@ -108,7 +108,8 @@
     def down_slice(r):
         return dw.at[0, :, pl.ds(pl.multiple_of(r * SLICE, SLICE), SLICE)]
 
-    downs = [send(down_slice(r), DT.at[rep], at_rep(r)) for r in rdev]
+    distant = [yy * C + cc for yy in (yo, yri, yl) for cc in (c, 1 - c)] + [y * C + 1 - c]
+    downs = [send(down_slice(r), DT.at[rep], at_rep(r)) for r in distant]
     own_down = pltpu.make_async_copy(down_slice(rep), DT.at[rep], lsem.at[2])
     own_down.start()
     SB[zhi, rep] = SA[rep]

time: 102 us -> 102 us (level)
  no operation moved by 1% of the time
where the time goes in v4:
time: 102 us
  Pallas kernels  100 us (98%)
  local copies, waits for them, and re-layouts  1.34 us (1%)
    pallas_call x1, Pallas kernels, on_device(): pl.pallas_call(kernel, out_shape=jax.ShapeDtypeStruct((COL // REP, D), bf...  100 us

profile of v4, /device:TPU:1, one launch (start us, length us, event | category | flops | bytes accessed | tf_op | source)
XLA Modules:
  0.0 101.7 jit_solution(15239171246195180157)
XLA Ops:
  0.0 100.3 %shard_map.73 = bf16[2,4096]{1,0:T(2,128)(2,1)} custom-call(bf16[2,4096]{1,0:T(2,128)(2,1)} %hid.1, f32[1,4096]{1,0:T(1,128)} %bitcast.3, s32[8,16]{1,0:T(8,128)} %bitcast.4, f32[8,16]{1,0:T(8,128)} %bitcast.5, bf16[1,4096,128]{2,1,0:T(8,128)(2,1)} %gw.1, bf16[1,4096,128]{2,1,0:T(8,128)(2,1)} %uw.1, bf16[1,128,4096]{2,1,0:T(8,128)(2,1)} %dw.1), custom_call_target="tpu_custom_call" | custom-call | tf_op jit(solution)/shard_map/pallas_call | solution.py:415
  100.3 1.3 %copy.9 = bf16[2,4096]{1,0:T(2,128)(2,1)} copy(bf16[2,4096]{1,0:T(2,128)(2,1)} %shard_map.73) | data formatting | bytes 32768
